TPU v7x, 256 devices: a whole 4x4x8 slice. The times are simulated.
256 devices in a mesh: ctx: 32 (over x, z), head: 8 (over y, core).
Axes of the slice: x: 4, y: 4, z: 8, core: 2. Of those that a mesh axis runs over, the one named last changes fastest.
Arguments:
- layer_input: bfloat16 [16384, 8192], P('ctx', 'head'), may hold values from -6 to 6
- query_columns: bfloat16 [16384, 8192], P('ctx', 'head'), may hold values from -6 to 6
- key_columns: bfloat16 [16384, 1024], P('ctx', 'head'), may hold values from -6 to 6
- value_columns: bfloat16 [16384, 1024], P('ctx', 'head'), may hold values from -6 to 6
- output_gradient: bfloat16 [16384, 8192], P('ctx', 'head'), may hold values from -6 to 6
Outputs:
- query_grad: bfloat16 [16384, 8192], P('ctx', 'head')
- key_weight_grad: float32 [8192, 1024], P(('head', 'ctx'))
- value_weight_grad: float32 [8192, 1024], P(('head', 'ctx'))
All inputs are finite; a program needn't handle non-finite values.
Results may differ from a plain program's by a relative error of at most 0.014.
Values may be sent and summed in bfloat16 or wider, within the bound.
A program may use at most 128 MiB of HBM per device.

v0:
```python
import jax
import jax.numpy as jnp
from jax import lax
from jax.sharding import PartitionSpec as P

QUERY_HEADS = 64
KEY_VALUE_HEADS = 8
HEAD_SIZE = 128
highest = lax.Precision.HIGHEST


def prefix(value, axis, combine, identity, reverse):
    devices, position = (lax.axis_size(axis), lax.axis_index(axis))
    everything = jax.tree.map(lambda part: lax.all_gather(part, axis), value)
    start = jax.tree.map(
        lambda part, zero: jnp.broadcast_to(jnp.asarray(zero, part.dtype), part.shape),
        value,
        identity,
    )

    def step(k, before):
        at = devices - 1 - k if reverse else k
        reached = at > position if reverse else at < position
        new = combine(before, jax.tree.map(lambda part: part[at], everything))
        return jax.tree.map(lambda a, b: jnp.where(reached, a, b), new, before)

    return lax.fori_loop(0, devices, step, start)


def positive_features(raw):
    wide = raw.astype(jnp.float32)
    return jnp.where(wide > 0, wide + 1.0, jnp.exp(jnp.minimum(wide, 0.0))).astype(jnp.bfloat16)


def feature_derivative(raw):
    wide = raw.astype(jnp.float32)
    return jnp.where(wide > 0, 1.0, jnp.exp(jnp.minimum(wide, 0.0)))


def causal_mask(length):
    rows_at = lax.broadcasted_iota(jnp.int32, (length, length), 0)
    cols_at = lax.broadcasted_iota(jnp.int32, (length, length), 1)
    return cols_at <= rows_at


def block_states(key_features, value_entries):
    states = jnp.einsum(
        "ske,skf->kef", key_features, value_entries, preferred_element_type=jnp.float32
    )
    totals = jnp.sum(key_features.astype(jnp.float32), axis=0)
    return (states, totals)


def block_scores(query_features, key_features):
    attention_scores = jnp.einsum(
        "tkge,ske->kgts", query_features, key_features, preferred_element_type=jnp.float32
    )
    return jnp.where(causal_mask(attention_scores.shape[-1]), attention_scores, jnp.float32(0.0))


def forward_blockwise_pass(
    query_features, value_entries, output_cotangent, prior_state, prior_total, attention_scores
):
    query_wide = query_features.astype(jnp.float32)
    denom = jnp.einsum("tkge,ke->tkg", query_wide, prior_total, precision=highest) + jnp.transpose(
        jnp.sum(attention_scores, axis=-1), (2, 0, 1)
    )
    numer = jnp.einsum("tkge,kef->tkgf", query_wide, prior_state, precision=highest) + jnp.einsum(
        "kgts,skf->tkgf",
        attention_scores.astype(jnp.bfloat16),
        value_entries,
        preferred_element_type=jnp.float32,
    )
    output = numer / denom[..., None]
    wide_cot = output_cotangent.astype(jnp.float32)
    scaled = (wide_cot / denom[..., None]).astype(jnp.bfloat16)
    weight = -jnp.sum(wide_cot * output, axis=-1) / denom
    grad_state = jnp.einsum(
        "tkge,tkgf->kef", query_features, scaled, preferred_element_type=jnp.float32
    )
    grad_total = jnp.einsum("tkge,tkg->ke", query_wide, weight, precision=highest)
    return (scaled, weight, grad_state, grad_total)


def backward_blockwise_pass(
    query_features,
    key_features,
    value_entries,
    lower_triangle_scores,
    scaled,
    weight,
    prior_state,
    prior_total,
    later_state,
    later_total,
):
    dscores = (
        jnp.einsum("tkgf,skf->kgts", scaled, value_entries, preferred_element_type=jnp.float32)
        + jnp.transpose(weight, (1, 2, 0))[..., None]
    )
    dscores = jnp.where(causal_mask(dscores.shape[-1]), dscores, jnp.float32(0.0)).astype(
        jnp.bfloat16
    )
    grad_query = (
        jnp.einsum("tkgf,kef->tkge", scaled.astype(jnp.float32), prior_state, precision=highest)
        + weight[..., None] * prior_total[None, :, None, :]
        + jnp.einsum("kgts,ske->tkge", dscores, key_features, preferred_element_type=jnp.float32)
    )
    key_gradient_rows = (
        jnp.einsum("kgts,tkge->ske", dscores, query_features, preferred_element_type=jnp.float32)
        + jnp.einsum(
            "kef,skf->ske", later_state, value_entries.astype(jnp.float32), precision=highest
        )
        + later_total[None]
    )
    value_gradient_rows = jnp.einsum(
        "kgts,tkgf->skf", lower_triangle_scores, scaled, preferred_element_type=jnp.float32
    ) + jnp.einsum("kef,ske->skf", later_state, key_features.astype(jnp.float32), precision=highest)
    return (grad_query, key_gradient_rows, value_gradient_rows)


def add_pair(earlier, later):
    return (earlier[0] + later[0], earlier[1] + later[1])


def shards(layer_input, query_columns, key_columns, value_columns, output_gradient):
    rows = query_columns.shape[0]
    local_kv = key_columns.shape[1] // HEAD_SIZE
    query_group_count = QUERY_HEADS // KEY_VALUE_HEADS
    block = min(256, rows)
    count = rows // block
    query_features = positive_features(query_columns).reshape(
        count, block, local_kv, query_group_count, HEAD_SIZE
    )
    key_features = positive_features(key_columns).reshape(count, block, local_kv, HEAD_SIZE)
    value_entries = value_columns.reshape(count, block, local_kv, HEAD_SIZE)
    output_cotangent = output_gradient.reshape(count, block, local_kv, query_group_count, HEAD_SIZE)
    pieces = [block_states(key_features[index], value_entries[index]) for index in range(count)]
    dev_state = pieces[0][0]
    dev_total = pieces[0][1]
    index = 1
    dev_state = dev_state + pieces[index][0]
    dev_total = dev_total + pieces[index][1]
    empty = (jnp.zeros_like(dev_state), jnp.zeros_like(dev_total))
    before_state, before_total = prefix((dev_state, dev_total), "ctx", add_pair, empty, False)
    priors = []
    running_state, running_total = (before_state, before_total)
    for index in range(count):
        priors.append((running_state, running_total))
        running_state = running_state + pieces[index][0]
        running_total = running_total + pieces[index][1]
    forwards = []
    for index in range(count):
        attention_scores = block_scores(query_features[index], key_features[index])
        forwards.append(
            forward_blockwise_pass(
                query_features[index],
                value_entries[index],
                output_cotangent[index],
                priors[index][0],
                priors[index][1],
                attention_scores,
            )
        )
    dev_gstate = forwards[0][2]
    dev_gtotal = forwards[0][3]
    index = 1
    dev_gstate = dev_gstate + forwards[index][2]
    dev_gtotal = dev_gtotal + forwards[index][3]
    after_state, after_total = prefix((dev_gstate, dev_gtotal), "ctx", add_pair, empty, True)
    laters = [None] * count
    running_state, running_total = (after_state, after_total)
    for index in range(count - 1, -1, -1):
        laters[index] = (running_state, running_total)
        running_state = running_state + forwards[index][2]
        running_total = running_total + forwards[index][3]
    query_parts = []
    key_parts = []
    value_parts = []
    for index in range(count):
        lower_triangle_scores = block_scores(query_features[index], key_features[index]).astype(
            jnp.bfloat16
        )
        grad_query, key_gradient_rows, value_gradient_rows = backward_blockwise_pass(
            query_features[index],
            key_features[index],
            value_entries[index],
            lower_triangle_scores,
            forwards[index][0],
            forwards[index][1],
            priors[index][0],
            priors[index][1],
            laters[index][0],
            laters[index][1],
        )
        query_parts.append(grad_query)
        key_parts.append(key_gradient_rows)
        value_parts.append(value_gradient_rows)
    query_grad = (
        jnp.concatenate(query_parts, axis=0).reshape(rows, query_columns.shape[1])
        * feature_derivative(query_columns)
    ).astype(jnp.bfloat16)
    key_gradient = (
        jnp.concatenate(key_parts, axis=0).reshape(rows, key_columns.shape[1])
        * feature_derivative(key_columns)
    ).astype(jnp.bfloat16)
    value_gradient = (
        jnp.concatenate(value_parts, axis=0)
        .reshape(rows, value_columns.shape[1])
        .astype(jnp.bfloat16)
    )
    key_all, value_all = (
        lax.all_gather(key_gradient, "head", axis=1, tiled=True),
        lax.all_gather(value_gradient, "head", axis=1, tiled=True),
    )
    joined = jnp.concatenate([key_all, value_all], axis=1)
    summed = lax.psum_scatter(
        jnp.einsum("tr,tc->rc", layer_input, joined, preferred_element_type=jnp.float32),
        "ctx",
        scatter_dimension=0,
        tiled=True,
    )
    half_width = key_all.shape[1]
    return (query_grad, summed[:, :half_width], summed[:, half_width:])


def solution(mesh):
    placed = (
        P("ctx", "head"),
        P("ctx", "head"),
        P("ctx", "head"),
        P("ctx", "head"),
        P("ctx", "head"),
    )
    return jax.shard_map(
        shards,
        mesh=mesh,
        in_specs=placed,
        out_specs=(P("ctx", "head"), P(("head", "ctx"), None), P(("head", "ctx"), None)),
        check_vma=False,
    )
```

profile of v0, /device:TPU:8, one launch (start us, length us, event | category | flops | bytes accessed | tf_op | source)
XLA Modules:
  0.0 587.1 jit_solution(2239093417903597590)
XLA Ops:
  9.3 1.7 convolution_add_fusion
  11.1 1.5 copy.102
  12.7 2.8 slice_convert_fusion.1
  15.5 2.5 copy.106
  18.0 1.3 copy.118
  19.4 41.8 %all-gather.5 = f32[32,1,128]{2,1,0:T(1,128)S(1)} all-gather(f32[1,1,128]{2,1,0:T(1,128)S(1)} %add_bitcast_fusion), channel_id=3, replica_groups=mesh['ctx'=32,'head'=8] {'ctx'}, dimensions={0}, use_global_device_ids=true | all-gather | bytes 16896 | tf_op jit(solution)/shard_map/all_gather | solution.py:14
  63.0 1.5 fusion.14
  64.5 27.5 %all-gather.14.cloned.1.call-done = f32[4096,128]{1,0:T(8,128)} async-done(((f32[128,128]{1,0:T(8,128)}), f32[4096,128]{1,0:T(8,128)}) %all-gather.14.cloned.1.call-update) | async-done | bytes 2097168 | tf_op jit(solution)/shard_map/all_gather | solution.py:14
  92.0 28.9 %while.34 = (s32[]{:T(128)}, f32[1,128,128]{2,1,0:T(8,128)S(1)}, f32[1,128]{1,0:T(1,128)S(1)}, s32[]{:T(128)}, f32[32,1,128,128]{3,2,1,0:T(8,128)}, /*index=5*/f32[32,1,128]{2,1,0:T(1,128)S(1)}, s32[]{:T(128)}, s32[]{:T(128)}) while((s32[]{:T(128)}, f32[1,128,128]{2,1,0:T(8,128)S(1)}, f32[1,128]{1,0:T(1,128)S(1)}, s32[]{:T(128)}, ...), condition=%wide.region_3.4_spmd.clone, body=%wide.region_2.3_spmd.clone.sunk | while | flops 49540 | bytes 198267 | solution.py:27
  120.9 2.7 fusion.105
  123.6 2.7 fusion.107
  126.3 1.5 copy.154
  127.9 1.6 copy.145
  129.5 1.4 divide_convert_fusion
  131.7 1.3 fusion.117
  134.2 2.6 convolution_bitcast_fusion.6
  136.8 1.4 convolution_bitcast_fusion.5
  139.2 2.6 copy.181
  142.8 2.6 copy.177
  145.4 2.5 fusion.30
  149.8 39.3 %all-gather.6 = f32[32,1,128]{2,1,0:T(1,128)} all-gather(f32[1,1,128]{2,1,0:T(1,128)S(1)} %fusion.41), channel_id=5, replica_groups=mesh['ctx'=32,'head'=8] {'ctx'}, dimensions={0}, use_global_device_ids=true | all-gather | bytes 16896 | tf_op jit(solution)/shard_map/all_gather | solution.py:14
  189.2 20.2 %all-gather.16.cloned.1.call-done = f32[4096,128]{1,0:T(8,128)} async-done(((f32[128,128]{1,0:T(8,128)}), f32[4096,128]{1,0:T(8,128)}) %all-gather.16.cloned.1.call-update) | async-done | bytes 2097168 | tf_op jit(solution)/shard_map/all_gather | solution.py:14
  209.4 66.8 %while.35 = (s32[]{:T(128)}, f32[1,128,128]{2,1,0:T(8,128)S(1)}, f32[1,128]{1,0:T(1,128)}, s32[]{:T(128)}, f32[32,1,128,128]{3,2,1,0:T(8,128)}, /*index=5*/f32[3...) while((s32[]{:T(128)}, f32[1,128,128]{2,1,0:T(8,128)S(1)}, f32[1,128]{1,0:T(1,128)}, ...), condition=%wide.region_9.10_spmd.clone, body=%wide.region_8.9_spmd.clone.sunk | while | flops 49544 | bytes 198329 | solution.py:27
  215.6 1.2 broadcast_select_fusion.7
  219.8 1.2 broadcast_select_fusion.7
  221.9 1.2 broadcast_select_fusion.7
  228.1 1.2 broadcast_select_fusion.7
  230.2 1.2 broadcast_select_fusion.7
  234.4 1.2 broadcast_select_fusion.7
  244.8 1.2 broadcast_select_fusion.7
  246.9 1.2 broadcast_select_fusion.7
  249.0 1.2 broadcast_select_fusion.7
  251.1 1.2 broadcast_select_fusion.7
  257.4 1.2 broadcast_select_fusion.7
  259.5 1.2 broadcast_select_fusion.7
  269.9 1.2 broadcast_select_fusion.7
  272.0 1.2 broadcast_select_fusion.7
  276.6 1.7 fusion.38
  279.9 1.6 fusion.48
  284.8 17.6 %all-gather.18.cloned.1.call-done = bf16[512,1,1024]{2,0,1:T(8,128)(2,1)} async-done(((bf16[512,1,128]{2,0,1:T(8,128)(2,1)}), bf16[512,1,1024]{2,0,1:T(8,128)(2,1)}) %all-gather.18.cloned.1.call-update) | async-done | bytes 1048592 | tf_op jit(solution)/shard_map/all_gather | solution.py:214
  302.4 29.2 %all-gather.12.cloned.1.call-done = bf16[512,1024]{1,0:T(8,128)(2,1)} async-done(((bf16[512,128]{1,0:T(8,128)(2,1)}), bf16[512,1024]{1,0:T(8,128)(2,1)}) %all-gather.12.cloned.1.call-update) | async-done | bytes 1048592 | tf_op jit(solution)/shard_map/all_gather | solution.py:213
  331.6 7.2 %convolution_bitcast_fusion = f32[1024,2048]{0,1:T(8,128)} fusion(bf16[512,1024]{1,0:T(8,128)(2,1)S(1)} %copy-done, bf16[512,1024]{1,0:T(8,128)(2,1)} %bitcast.434, bf16[512,1024]{1,0:T(8,128)(2,1)} %all-gather.12.cloned.1.call-done), kind=kOutput, calls=%fused_computation.6 | convolution fusion | flops 2151677952 | bytes 11534336 | tf_op jit(solution)/shard_map/tr,tc->rc/dot_general | solution.py:218
  338.8 9.2 %copy.191 = f32[1024,2048]{1,0:T(8,128)} copy(f32[1024,2048]{0,1:T(8,128)} %convolution_bitcast_fusion) | data formatting | bytes 16777216
  348.0 1.2 copy-done.14
  352.9 1.5 fusion.5
  354.4 2.3 copy.142
  356.6 222.3 %reduce-scatter.4.cloned.1.call-done = f32[32,2048]{1,0:T(8,128)} async-done(((f32[1024,2048]{1,0:T(8,128)}), f32[32,2048]{1,0:T(8,128)}) %reduce-scatter.4.cloned.1.call-update) | async-done | bytes 262160
  578.9 1.7 fusion.116
  (256 shorter events, 95.3 us)
Async XLA Ops:
  7.2 324.5 %copy-start = (bf16[512,1024]{1,0:T(8,128)(2,1)S(1)}, bf16[512,1024]{1,0:T(8,128)(2,1)}, u32[]{:S(2)}) copy-start(bf16[512,1024]{1,0:T(8,128)(2,1)} %param.9) | copy-start | bytes 3145732
  7.2 84.8 %all-gather.14.cloned.1.call-start = ((), (), s32[]{:S(2)}) async-start(), calls=%async_computation.2 | async-start | bytes 2162688 | tf_op jit(solution)/shard_map/all_gather | solution.py:14
  9.3 1.8 copy-start.26
  11.1 198.3 %all-gather.16.cloned.1.call-start = ((), (), s32[]{:S(2)}) async-start(), calls=%async_computation.3 | async-start | bytes 2162688 | tf_op jit(solution)/shard_map/all_gather | solution.py:14
  12.6 48.6 %copy-start.8 = (bf16[512,1024]{0,1:T(8,128)(2,1)}, bf16[512,1024]{0,1:T(8,128)(2,1)S(1)}, u32[]{:S(2)}) copy-start(bf16[512,1024]{0,1:T(8,128)(2,1)S(1)} %copy.102) | copy-start | bytes 3145732
  19.4 101.5 %copy-start.43 = (f32[128]{0:T(128)}, f32[128]{0:T(128)S(1)}, u32[]{:S(2)}) copy-start(f32[128]{0:T(128)S(1)} %get-tuple-element.360) | copy-start | bytes 1540
  61.8 0.8 copy-start.1
  61.8 1.2 copy-start.4
  64.5 64.9 %copy-start.32 = (f32[8,256]{1,0:T(8,128)}, f32[8,256]{1,0:T(8,128)S(1)}, u32[]{:S(2)}) copy-start(f32[8,256]{1,0:T(8,128)S(1)} %get-tuple-element.362) | copy-start | bytes 24580
  64.5 68.5 %copy-start.30 = (f32[8,256]{1,0:T(8,128)}, f32[8,256]{1,0:T(8,128)S(1)}, u32[]{:S(2)}) copy-start(f32[8,256]{1,0:T(8,128)S(1)} %get-tuple-element.361) | copy-start | bytes 24580
  120.9 2.7 copy-start.40
  127.9 6.2 %copy-start.34 = (f32[1,256,8]{1,2,0:T(8,128)}, f32[1,256,8]{1,2,0:T(8,128)S(1)}, u32[]{:S(2)}) copy-start(f32[1,256,8]{1,2,0:T(8,128)S(1)} %copy.154) | copy-start | bytes 24580
  129.4 4.6 copy-start.36
  129.4 3.7 copy-start.5
  129.5 3.7 copy-start.24
  130.9 0.8 copy-start.10
  133.1 12.3 %copy-start.38 = (f32[256,8]{0,1:T(8,128)}, f32[256,8]{0,1:T(8,128)S(1)}, u32[]{:S(2)}) copy-start(f32[256,8]{0,1:T(8,128)S(1)} %fusion.102) | copy-start | bytes 24580
  134.1 168.3 %all-gather.18.cloned.1.call-start = ((), (), s32[]{:S(2)}) async-start(), calls=%async_computation.4 | async-start | bytes 1179648 | tf_op jit(solution)/shard_map/all_gather | solution.py:214
  134.2 2.6 copy-start.21
  145.4 2.6 copy-start.2
  145.4 2.6 copy-start.12
  145.4 2.6 copy-start.23
  145.4 2.6 copy-start.27
  148.0 0.8 copy-start.31
  148.0 0.8 copy-start.33
  148.0 0.8 copy-start.35
  148.0 1.3 copy-start.6
  276.2 2.1 copy-start.15
  276.2 2.1 copy-start.25
  276.2 2.1 copy-start.39
  278.3 1.4 copy-start.11
  278.3 1.6 copy-start.16
  279.5 52.1 %all-gather.12.cloned.1.call-start = ((), (), s32[]{:S(2)}) async-start(), calls=%async_computation.1 | async-start | bytes 1179648 | tf_op jit(solution)/shard_map/all_gather | solution.py:213
  279.9 1.6 copy-start.22
  281.5 1.0 copy-start.17
  281.5 1.0 copy-start.19
  281.6 1.5 copy-start.42
  281.6 1.5 copy-start.46
  281.6 1.5 copy-start.7
  282.0 1.5 copy-start.13
  282.1 1.5 copy-start.3
  282.5 1.4 copy-start.29
  284.7 294.2 %reduce-scatter.4.cloned.1.call-start = ((), (), s32[]{:S(2)}) async-start(), calls=%async_computation.5 | async-start | bytes 8650752
  348.0 1.2 copy-start.14
  349.2 1.0 copy-start.20
  349.6 1.4 copy-start.18
  349.6 1.4 copy-start.28
  351.6 1.2 copy-start.9
  (4 other events, 2.7 us)
Sparse Core Ops, SparseCore 0:
  11.2 80.7 all-gather.13
  134.2 75.1 all-gather.15
  279.6 22.7 all-gather.17
  304.7 26.9 all-gather.11
  348.1 230.7 reduce-scatter.3
where the time goes:
time: 591 us; the launch traced here: 587 us
  waiting for transfers between devices  317 us (54%)
  other arithmetic  105 us (18%)
  blocking collectives  81.1 us (14%)
  matrix products  34.4 us (6%)
  local copies, waits for them, and re-layouts  33.4 us (6%)
  between operations  14.6 us (2%)
    unnamed x6, waiting for transfers between devices  222 us
    select_n x128, other arithmetic, step(): return jax.tree.map(lambda a, b: jnp.where(reached, a, b), new, before)  93.9 us
    all_gather x2, blocking collectives, prefix(): everything = jax.tree.map(lambda part: lax.all_gather(part, axis), value)  81.1 us
    all_gather x2, waiting for transfers between devices, prefix(): everything = jax.tree.map(lambda part: lax.all_gather(part, axis), value)  47.7 us
    all_gather x1, waiting for transfers between devices, shards(): lax.all_gather(key_gradient, 'head', axis=1, tiled=True)  29.2 us
    all_gather x1, waiting for transfers between devices, shards(): lax.all_gather(value_gradient, 'head', axis=1, tiled=True)  17.6 us
    unnamed x97, local copies, waits for them, and re-layouts  17.5 us
  transfers between devices with their start and end apart: 5, of which 5 were waited for; matrix products, arithmetic and copies ran while one was open for 6% of the time, Pallas kernels for 0%

commit v1 on v0

--- a/solution.py
+++ b/solution.py
@@ -210,7 +210,9 @@
         .astype(jnp.bfloat16)
     )
     key_all, value_all = (
-        lax.all_gather(key_gradient, "head", axis=1, tiled=True),
+        jnp.concatenate(
+            lax.all_to_all(jnp.stack([key_gradient] * lax.axis_size("head")), "head", 0, 0), axis=1
+        ),
         lax.all_gather(value_gradient, "head", axis=1, tiled=True),
     )
     joined = jnp.concatenate([key_all, value_all], axis=1)

time: 591 us -> 566 us (0.958)
  waiting for transfers between devices: 317 us -> 263 us
  blocking collectives: 81.1 us -> 105 us
    all_gather x1 -> x0, waiting for transfers between devices: 29.2 us -> none  [shards(): lax.all_gather(key_gradient, 'head', axis=1, tiled=True)]
    all_to_all x0 -> x1, blocking collectives: none -> 23.5 us  [shards(): lax.all_to_all(jnp.stack([key_gradient] * lax.axis_size('head')), 'head',...]
    all_gather x1, waiting for transfers between devices: 17.6 us -> 0.01 us  [shards(): lax.all_gather(value_gradient, 'head', axis=1, tiled=True)]
    unnamed x6 -> x5, waiting for transfers between devices: 222 us -> 219 us
  transfers between devices with their start and end apart: 5 -> 4, of which waited for: 5 -> 3; matrix products, arithmetic and copies ran while one was open for 6% -> 7% of each run, Pallas kernels for 0% -> 0%
where the time goes in v1:
time: 566 us; the launch traced here: 562 us
  waiting for transfers between devices  263 us (46%)
  blocking collectives  105 us (19%)
  other arithmetic  104 us (18%)
  matrix products  39.4 us (7%)
  local copies, waits for them, and re-layouts  34.1 us (6%)
  between operations  14.6 us (3%)
    unnamed x5, waiting for transfers between devices  219 us
    select_n x128, other arithmetic, step(): return jax.tree.map(lambda a, b: jnp.where(reached, a, b), new, before)  93.9 us
    all_gather x2, blocking collectives, prefix(): everything = jax.tree.map(lambda part: lax.all_gather(part, axis), value)  81.2 us
    all_gather x2, waiting for transfers between devices, prefix(): everything = jax.tree.map(lambda part: lax.all_gather(part, axis), value)  43.4 us
    all_to_all x1, blocking collectives, shards(): lax.all_to_all(jnp.stack([key_gradient] * lax.axis_size('head')), 'head',...  23.5 us
    unnamed x97, local copies, waits for them, and re-layouts  18.1 us
  transfers between devices with their start and end apart: 4, of which 3 were waited for; matrix products, arithmetic and copies ran while one was open for 7% of the time, Pallas kernels for 0%

profile of v1, /device:TPU:8, one launch (start us, length us, event | category | flops | bytes accessed | tf_op | source)
XLA Modules:
  0.0 561.7 jit_solution(15373087524890025800)
XLA Ops:
  9.3 1.7 convolution_add_fusion
  11.1 1.5 copy.104
  12.7 2.8 slice_convert_fusion.1
  15.5 2.5 copy.108
  18.0 1.3 copy.120
  19.4 41.8 %all-gather.5 = f32[32,1,128]{2,1,0:T(1,128)S(1)} all-gather(f32[1,1,128]{2,1,0:T(1,128)S(1)} %add_bitcast_fusion), channel_id=3, replica_groups=mesh['ctx'=32,'head'=8] {'ctx'}, dimensions={0}, use_global_device_ids=true | all-gather | bytes 16896 | tf_op jit(solution)/shard_map/all_gather | solution.py:14
  63.0 1.5 fusion.14
  64.5 27.5 %all-gather.11.cloned.1.call-done = f32[4096,128]{1,0:T(8,128)} async-done(((f32[128,128]{1,0:T(8,128)}), f32[4096,128]{1,0:T(8,128)}) %all-gather.11.cloned.1.call-update) | async-done | bytes 2097168 | tf_op jit(solution)/shard_map/all_gather | solution.py:14
  92.0 28.9 %while.34 = (s32[]{:T(128)}, f32[1,128,128]{2,1,0:T(8,128)S(1)}, f32[1,128]{1,0:T(1,128)S(1)}, s32[]{:T(128)}, f32[32,1,128,128]{3,2,1,0:T(8,128)}, /*index=5*/f32[32,1,128]{2,1,0:T(1,128)S(1)}, s32[]{:T(128)}, s32[]{:T(128)}) while((s32[]{:T(128)}, f32[1,128,128]{2,1,0:T(8,128)S(1)}, f32[1,128]{1,0:T(1,128)S(1)}, s32[]{:T(128)}, ...), condition=%wide.region_3.4_spmd.clone, body=%wide.region_2.3_spmd.clone.sunk | while | flops 49540 | bytes 198267 | solution.py:27
  120.9 2.7 fusion.105
  123.6 2.7 fusion.107
  126.3 1.5 copy.157
  127.9 1.6 copy.148
  129.5 1.4 divide_convert_fusion
  131.7 1.3 fusion.117
  134.2 2.6 convolution_bitcast_fusion.6
  136.8 1.4 convolution_bitcast_fusion.5
  139.2 2.5 copy.184
  142.8 2.5 copy.180
  145.3 2.5 fusion.30
  149.9 39.5 %all-gather.6 = f32[32,1,128]{2,1,0:T(1,128)} all-gather(f32[1,1,128]{2,1,0:T(1,128)S(1)} %fusion.41), channel_id=5, replica_groups=mesh['ctx'=32,'head'=8] {'ctx'}, dimensions={0}, use_global_device_ids=true | all-gather | bytes 16896 | tf_op jit(solution)/shard_map/all_gather | solution.py:14
  190.5 1.4 fusion.17
  192.0 1.4 fusion.18
  193.4 16.0 %all-gather.13.cloned.1.call-done = f32[4096,128]{1,0:T(8,128)} async-done(((f32[128,128]{1,0:T(8,128)}), f32[4096,128]{1,0:T(8,128)}) %all-gather.13.cloned.1.call-update) | async-done | bytes 2097168 | tf_op jit(solution)/shard_map/all_gather | solution.py:14
  209.4 66.8 %while.35 = (s32[]{:T(128)}, f32[1,128,128]{2,1,0:T(8,128)S(1)}, f32[1,128]{1,0:T(1,128)}, s32[]{:T(128)}, f32[32,1,128,128]{3,2,1,0:T(8,128)}, /*index=5*/f32[3...) while((s32[]{:T(128)}, f32[1,128,128]{2,1,0:T(8,128)S(1)}, f32[1,128]{1,0:T(1,128)}, ...), condition=%wide.region_9.10_spmd.clone, body=%wide.region_8.9_spmd.clone.sunk | while | flops 49544 | bytes 198329 | solution.py:27
  211.4 1.2 broadcast_select_fusion.7
  213.5 1.2 broadcast_select_fusion.7
  215.6 1.2 broadcast_select_fusion.7
  224.0 1.2 broadcast_select_fusion.7
  226.1 1.2 broadcast_select_fusion.7
  228.2 1.2 broadcast_select_fusion.7
  232.4 1.2 broadcast_select_fusion.7
  242.8 1.2 broadcast_select_fusion.7
  249.1 1.2 broadcast_select_fusion.7
  253.2 1.2 broadcast_select_fusion.7
  255.3 1.2 broadcast_select_fusion.7
  269.9 1.2 broadcast_select_fusion.7
  274.1 1.2 broadcast_select_fusion.7
  276.7 1.3 fusion.104
  278.1 1.5 fusion.38
  283.3 1.7 fusion.36
  285.7 23.5 %all_to_all.5 = bf16[8,512,128]{1,2,0:T(8,128)(2,1)} all-to-all(bf16[8,512,128]{1,2,0:T(8,128)(2,1)S(1)} %stack.2), channel_id=1, replica_groups=mesh['ctx'=32,'head'=8] {'head'}, dimensions={0} | all-to-all | bytes 2097152 | tf_op jit(solution)/shard_map/all_to_all | solution.py:214
  309.2 7.1 %convolution_bitcast_fusion = f32[1024,2048]{0,1:T(8,128)} fusion(bf16[512,1024]{1,0:T(8,128)(2,1)S(1)} %copy-done, bf16[512,1024]{0,1:T(8,128)(2,1)} %bitcast.438, bf16[512,1024]{0,1:T(8,128)(2,1)} %bitcast.427), kind=kOutput, calls=%fused_computation.6 | convolution fusion | flops 2151677952 | bytes 11534336 | tf_op jit(solution)/shard_map/tr,tc->rc/dot_general | solution.py:220
  316.4 9.2 %copy.192 = f32[1024,2048]{1,0:T(8,128)} copy(f32[1024,2048]{0,1:T(8,128)} %convolution_bitcast_fusion) | data formatting | bytes 16777216
  330.4 1.5 fusion.5
  331.9 2.3 copy.145
  334.2 219.2 %reduce-scatter.4.cloned.1.call-done = f32[32,2048]{1,0:T(8,128)} async-done(((f32[1024,2048]{1,0:T(8,128)}), f32[32,2048]{1,0:T(8,128)}) %reduce-scatter.4.cloned.1.call-update) | async-done | bytes 262160
  553.4 1.7 fusion.116
  (256 shorter events, 98.6 us)
Async XLA Ops:
  7.2 302.1 %copy-start = (bf16[512,1024]{1,0:T(8,128)(2,1)S(1)}, bf16[512,1024]{1,0:T(8,128)(2,1)}, u32[]{:S(2)}) copy-start(bf16[512,1024]{1,0:T(8,128)(2,1)} %param.9) | copy-start | bytes 3145732
  7.2 84.8 %all-gather.11.cloned.1.call-start = ((), (), s32[]{:S(2)}) async-start(), calls=%async_computation.2 | async-start | bytes 2162688 | tf_op jit(solution)/shard_map/all_gather | solution.py:14
  9.3 1.8 copy-start.27
  11.1 198.3 %all-gather.13.cloned.1.call-start = ((), (), s32[]{:S(2)}) async-start(), calls=%async_computation.3 | async-start | bytes 2162688 | tf_op jit(solution)/shard_map/all_gather | solution.py:14
  12.6 48.6 %copy-start.8 = (bf16[512,1024]{0,1:T(8,128)(2,1)}, bf16[512,1024]{0,1:T(8,128)(2,1)S(1)}, u32[]{:S(2)}) copy-start(bf16[512,1024]{0,1:T(8,128)(2,1)S(1)} %copy.104) | copy-start | bytes 3145732
  19.4 101.5 %copy-start.44 = (f32[128]{0:T(128)}, f32[128]{0:T(128)S(1)}, u32[]{:S(2)}) copy-start(f32[128]{0:T(128)S(1)} %get-tuple-element.360) | copy-start | bytes 1540
  61.8 0.8 copy-start.1
  61.8 1.2 copy-start.4
  64.5 65.0 %copy-start.33 = (f32[8,256]{1,0:T(8,128)}, f32[8,256]{1,0:T(8,128)S(1)}, u32[]{:S(2)}) copy-start(f32[8,256]{1,0:T(8,128)S(1)} %get-tuple-element.362) | copy-start | bytes 24580
  64.5 68.5 %copy-start.31 = (f32[8,256]{1,0:T(8,128)}, f32[8,256]{1,0:T(8,128)S(1)}, u32[]{:S(2)}) copy-start(f32[8,256]{1,0:T(8,128)S(1)} %get-tuple-element.361) | copy-start | bytes 24580
  120.9 2.7 copy-start.41
  127.9 6.2 %copy-start.35 = (f32[1,256,8]{1,2,0:T(8,128)}, f32[1,256,8]{1,2,0:T(8,128)S(1)}, u32[]{:S(2)}) copy-start(f32[1,256,8]{1,2,0:T(8,128)S(1)} %copy.157) | copy-start | bytes 24580
  129.5 4.6 copy-start.37
  129.5 3.6 copy-start.5
  129.5 3.6 copy-start.25
  130.9 0.8 copy-start.10
  133.1 12.2 %copy-start.39 = (f32[256,8]{0,1:T(8,128)}, f32[256,8]{0,1:T(8,128)S(1)}, u32[]{:S(2)}) copy-start(f32[256,8]{0,1:T(8,128)S(1)} %fusion.102) | copy-start | bytes 24580
  134.1 175.1 %all-gather.15.cloned.1.call-start = ((), (), s32[]{:S(2)}) async-start(), calls=%async_computation.4 | async-start | bytes 1179648 | tf_op jit(solution)/shard_map/all_gather | solution.py:216
  134.2 2.6 copy-start.22
  145.3 2.6 copy-start.2
  145.3 2.6 copy-start.14
  145.3 2.6 copy-start.24
  145.3 2.6 copy-start.28
  147.9 0.8 copy-start.32
  147.9 0.8 copy-start.34
  147.9 0.8 copy-start.36
  147.9 0.8 copy-start.38
  148.0 1.3 copy-start.6
  148.0 41.4 %copy-start.11 = (bf16[512,1024]{1,0:T(8,128)(2,1)S(1)}, bf16[512,1024]{1,0:T(8,128)(2,1)}, u32[]{:S(2)}) copy-start(bf16[512,1024]{1,0:T(8,128)(2,1)} %param.13) | copy-start | bytes 3145732
  148.0 41.4 %copy-start.16 = (f32[256,1024]{1,0:T(8,128)S(1)}, f32[256,1024]{1,0:T(8,128)}, u32[]{:S(2)}) copy-start(f32[256,1024]{1,0:T(8,128)} %copy.184) | copy-start | bytes 3145732
  148.0 41.4 %copy-start.17 = (f32[256,1024]{1,0:T(8,128)S(1)}, f32[256,1024]{1,0:T(8,128)}, u32[]{:S(2)}) copy-start(f32[256,1024]{1,0:T(8,128)} %copy.180) | copy-start | bytes 3145732
  189.3 1.2 copy-start.23
  189.7 0.8 copy-start.20
  189.7 2.3 copy-start.18
  276.2 3.4 copy-start.15
  276.2 3.4 copy-start.26
  276.2 3.4 copy-start.40
  279.6 3.7 copy-start.7
  280.1 4.8 copy-start.3
  280.1 4.8 copy-start.12
  280.1 4.8 copy-start.43
  280.8 272.6 %reduce-scatter.4.cloned.1.call-start = ((), (), s32[]{:S(2)}) async-start(), calls=%async_computation.5 | async-start | bytes 8650752
  281.1 4.4 copy-start.30
  325.6 1.2 copy-start.13
  326.8 1.0 copy-start.21
  327.1 1.4 copy-start.19
  327.1 1.4 copy-start.29
  329.2 1.2 copy-start.9
  (3 other events, 2.0 us)
Sparse Core Ops, SparseCore 0:
  11.2 80.7 all-gather.10
  134.2 75.1 all-gather.12
  281.0 25.8 all-gather.14
  325.7 227.6 reduce-scatter.3
